TPU v7x, 128 devices: a whole 4x4x4 slice. The times are simulated.
128 devices in a mesh: ctx: 16 (over y, x_lo, core), head: 8 (over z, x_hi).
Axes of the slice: x: 4 (x_hi: 2, x_lo: 2; x = x_hi * 2 + x_lo), y: 4, z: 4, core: 2. Of those that a mesh axis runs over, the one named last changes fastest.
Arguments:
- q_prompt: bfloat16 [8192, 32, 256], P('ctx', 'head'), may hold values from -0.3984375 to 0.3984375
- k_prompt: bfloat16 [8192, 32, 256], P('ctx', 'head'), may hold values from -0.3984375 to 0.3984375
- v_prompt: bfloat16 [8192, 32, 256], P('ctx', 'head'), may hold values from -6 to 6
- log_decay: float32 [32, 8192], P('head', 'ctx'), may hold values from -1 to 0
- prompt_section: int32 [512, 1], P('ctx'), may hold values from 0 to 15; in each aligned block of 32 rows (0 to 31, 32 to 63, ...) at most 4 rows name the same one
- q_step: bfloat16 [512, 4, 32, 256], P('ctx', None, 'head'), may hold values from -0.3984375 to 0.3984375
- k_step: bfloat16 [512, 4, 32, 256], P('ctx', None, 'head'), may hold values from -3 to 3
- v_step: bfloat16 [512, 4, 32, 256], P('ctx', None, 'head'), may hold values from -6 to 6
- step_decay: float32 [32, 4, 512], P('head', None, 'ctx'), may hold values from -0.6 to -0.05
- w_out: bfloat16 [8192, 8192], P(None, 'head'), may hold values from -0.0625 to 0.0625
Outputs:
- prompt_out: bfloat16 [8192, 8192], P('ctx', 'head')
- step_out: bfloat16 [512, 4, 8192], P('ctx', None, 'head')
Inputs may be any that keep to these rules, and one draw needn't show every extreme that they name: `prompt_section`: among the rows of one index of ctx, no section is named more than 4 times.
All inputs are finite; a program needn't handle non-finite values.
Results may differ from a plain program's by a relative error of at most 0.015.
Values may be sent and summed in bfloat16 or wider, within the bound.
No kernel may reach another device: no remote copies, remote signals or barrier semaphores. Data moves between devices by JAX's collectives and lax.ppermute only.
A program may use at most 128 MiB of HBM per device.

v0:
```python
import jax
import jax.numpy as jnp
from jax import lax
from jax.sharding import PartitionSpec as P

CAP = 4


def entering(value, axis, join, neutral):
    count, mine = (lax.axis_size(axis), lax.axis_index(axis))
    pieces = jax.tree.map(lambda part: lax.all_gather(part, axis), value)
    running = jax.tree.map(
        lambda part, zero: jnp.full_like(part, 0) + jnp.asarray(zero, part.dtype), value, neutral
    )

    def step(position, running):
        longer = join(running, jax.tree.map(lambda part: part[position], pieces))
        return jax.tree.map(lambda new, old: jnp.where(position < mine, new, old), longer, running)

    return lax.fori_loop(0, count - 1, step, running)


def as_sent(value):
    return jax.tree.map(lambda a: a.astype(jnp.bfloat16) if a.dtype == jnp.float32 else a, value)


def split_state(state):
    high_part = state.astype(jnp.bfloat16)
    rest = state - lax.optimization_barrier(high_part).astype(jnp.float32)
    middle_part = rest.astype(jnp.bfloat16)
    low_part = (rest - lax.optimization_barrier(middle_part).astype(jnp.float32)).astype(
        jnp.bfloat16
    )
    return (high_part, middle_part, low_part)


def exact_read(form, query_rows, state):
    parts = split_state(state)
    total = jnp.einsum(form, query_rows, parts[0], preferred_element_type=jnp.float32)
    total = total + jnp.einsum(form, query_rows, parts[1], preferred_element_type=jnp.float32)
    return total + jnp.einsum(form, query_rows, parts[2], preferred_element_type=jnp.float32)


def block_terms(carry_state, query_rows, key_matrix_rows, value_rows, log_rates):
    positions = jnp.arange(log_rates.shape[1])
    causal = positions[:, None] >= positions[None, :]
    cumlog = jnp.cumsum(log_rates, axis=1)
    decays = jnp.where(
        causal[None], jnp.exp(jnp.minimum(cumlog[:, :, None] - cumlog[:, None, :], 0.0)), 0.0
    )
    attention_scores = jnp.einsum(
        "jsv,csv->sjc", query_rows, key_matrix_rows, preferred_element_type=jnp.float32
    )
    weights = (attention_scores * decays).astype(jnp.bfloat16)
    within = jnp.einsum("hnm,mhe->nhe", weights, value_rows, preferred_element_type=jnp.float32)
    carried = exact_read("nhd,hde->nhe", query_rows, carry_state)
    carried = carried * jnp.exp(cumlog).T[:, :, None]
    last_log = cumlog[:, -1]
    weighted_values = (
        key_matrix_rows.astype(jnp.float32) * jnp.exp(last_log[:, None] - cumlog).T[:, :, None]
    ).astype(jnp.bfloat16)
    state_update = jnp.einsum(
        "jxa,jxp->xap", weighted_values, value_rows, preferred_element_type=jnp.float32
    )
    carry_state = jnp.exp(last_log)[:, None, None] * carry_state + state_update
    return (carry_state, within + carried, cumlog)


def combine(earlier, latter):
    return (earlier[0] + latter[0], jnp.exp(latter[0])[:, None, None] * earlier[1] + latter[1])


def shards(
    q_prompt,
    k_prompt,
    v_prompt,
    log_decay,
    prompt_section,
    q_step,
    k_step,
    v_step,
    step_decay,
    w_out,
):
    token_count, heads_here, head_dim = q_prompt.shape
    sections = lax.axis_size("ctx")
    carry_state = jnp.zeros((heads_here, head_dim, head_dim), jnp.float32)
    carry_state, partial_value, cumlog = block_terms(
        carry_state, q_prompt, k_prompt, v_prompt, log_decay
    )
    offset = cumlog[:, -1]
    identity = (jnp.zeros_like(offset), jnp.zeros_like(carry_state))
    earlier_log, entry_state = entering((offset, carry_state), "ctx", combine, identity)
    entry_parts = split_state(entry_state)
    entry_read = jnp.einsum(
        "nhd,hde->nhe", q_prompt, entry_parts[0], preferred_element_type=jnp.float32
    )
    entry_read = entry_read + jnp.einsum(
        "nhd,hde->nhe", q_prompt, entry_parts[1], preferred_element_type=jnp.float32
    )
    entry_read = entry_read + jnp.einsum(
        "nhd,hde->nhe", q_prompt, entry_parts[2], preferred_element_type=jnp.float32
    )
    block_out = partial_value + jnp.exp(cumlog).T[:, :, None] * entry_read
    retained = block_out.astype(jnp.bfloat16)
    retention = retained.reshape(token_count, heads_here * head_dim)

    def project_into(shard_piece):
        return jnp.dot(shard_piece, w_out, preferred_element_type=jnp.float32)

    prompt_out = project_into(lax.all_gather(retention, "head", axis=1, tiled=True))
    prompt_out = prompt_out.astype(jnp.bfloat16)
    final_state = jnp.exp(offset)[:, None, None] * entry_state + carry_state
    row_count, step_count = (q_step.shape[0], q_step.shape[1])
    section_ids = prompt_section[:, 0]
    owner_hot = (section_ids[:, None] == jnp.arange(sections)[None, :]).astype(jnp.float32)
    before = jnp.tril(jnp.ones((row_count, row_count), jnp.float32), -1)
    counts_before = jnp.dot(before, owner_hot, precision=lax.Precision.HIGHEST)
    ranking = jnp.sum(counts_before * owner_hot, axis=1).astype(jnp.int32)
    slot_ids = section_ids * CAP + ranking
    selector = (jnp.arange(sections * CAP)[:, None] == slot_ids[None, :]).astype(jnp.bfloat16)
    packed = jnp.dot(selector, q_step.reshape(row_count, -1), preferred_element_type=jnp.float32)
    packed = packed.astype(jnp.bfloat16).reshape(sections, CAP, step_count, heads_here, head_dim)
    reads = exact_read(
        "jcthd,jhde->jcthe",
        packed,
        lax.all_gather(as_sent(final_state[None]), "ctx", axis=0, tiled=True),
    )
    slot_reads = reads
    slot_reads = slot_reads.reshape(sections * CAP, step_count, heads_here, head_dim)
    prefix_reads = jnp.take(slot_reads, slot_ids, axis=0)
    step_logs = jnp.cumsum(jnp.transpose(step_decay, (2, 1, 0)), axis=1)
    head_logs = jnp.transpose(step_logs, (0, 2, 1))
    step_index = jnp.arange(step_count)
    causal = step_index[:, None] >= step_index[None, :]
    step_weights = jnp.where(
        causal[None, None],
        jnp.exp(jnp.minimum(head_logs[:, :, :, None] - head_logs[:, :, None, :], 0.0)),
        0.0,
    )
    attention_scores = jnp.einsum(
        "rthd,ruhd->rhtu", q_step, k_step, preferred_element_type=jnp.float32
    )
    own_terms = jnp.einsum(
        "rhtu,ruhe->rthe", attention_scores * step_weights, v_step.astype(jnp.float32)
    )
    step_retention = (jnp.exp(step_logs)[:, :, :, None] * prefix_reads + own_terms).astype(
        jnp.bfloat16
    )
    step_flat = step_retention.reshape(row_count * step_count, heads_here * head_dim)
    step_out = project_into(lax.all_gather(step_flat, "head", axis=1, tiled=True))
    step_out = step_out.astype(jnp.bfloat16).reshape(row_count, step_count, w_out.shape[1])
    return (prompt_out, step_out)


def solution(mesh):
    in_specs = (
        P("ctx", "head", None),
        P("ctx", "head", None),
        P("ctx", "head", None),
        P("head", "ctx"),
        P("ctx", None),
        P("ctx", None, "head", None),
        P("ctx", None, "head", None),
        P("ctx", None, "head", None),
        P("head", None, "ctx"),
        P(None, "head"),
    )
    out_specs = (P("ctx", "head"), P("ctx", None, "head"))
    return jax.shard_map(shards, mesh=mesh, in_specs=in_specs, out_specs=out_specs, check_vma=False)
```

profile of v0, /device:TPU:1, one launch (start us, length us, event | category | flops | bytes accessed | tf_op | source)
XLA Modules:
  0.0 372.0 jit_solution(12672800232312546022)
XLA Ops:
  7.2 0.8 reshape.123
  8.0 1.2 reduce-window.6
  10.1 1.8 multiply_convert_fusion.1
  11.8 1.2 dynamic-slice
  13.8 1.5 convolution_add_fusion
  15.5 28.4 %all-reduce = f32[64]{0:T(128)S(1)} all-reduce(f32[64]{0:T(128)S(1)} %get-tuple-element.133), channel_id=2, replica_groups=mesh['ctx'=16,'head'=8] {'ctx'}, use_global_device_ids=true, to_apply=%add | all-reduce | flops 64 | bytes 512
  44.0 66.9 %all-gather.12.cloned.1.call-done = f32[64,256,256]{2,1,0:T(8,128)} async-done(((f32[4,256,256]{2,1,0:T(8,128)}), f32[64,256,256]{2,1,0:T(8,128)}) %all-gather.12.cloned.1.call-update) | async-done | bytes 16777232 | tf_op jit(solution)/shard_map/all_gather | solution.py:11
  110.9 24.1 %while.14 = (s32[]{:T(128)}, f32[4,256,256]{2,1,0:T(8,128)S(1)}, s32[]{:T(128)}, f32[16,4]{1,0:T(8,128)S(1)}, f32[16,4,256,256]{3,2,1,0:T(8,128)}, /*index=5*/s32[]{:T(128)}, s32[]{:T(128)}) while((s32[]{:T(128)}, f32[4,256,256]{2,1,0:T(8,128)S(1)}, s32[]{:T(128)}, f32[16,4]{1,0:T(8,128)S(1)}, f32[16,4,256,256]{3,2,1,0:T(8,128)}, ...), condition=%wide.region_3.4_spmd.clone, body=%wide.region_2.3_spmd.clone.sunk | while | flops 1048580 | bytes 3145881 | solution.py:20
  110.9 1.6 fusion.85
  112.5 1.6 fusion.85
  114.1 1.6 fusion.85
  115.7 1.6 fusion.85
  117.4 1.6 fusion.85
  119.0 1.6 fusion.85
  120.6 1.6 fusion.85
  122.2 1.6 fusion.85
  123.8 1.6 fusion.85
  125.4 1.6 fusion.85
  127.0 1.6 fusion.85
  128.6 1.6 fusion.85
  130.2 1.6 fusion.85
  131.8 1.6 fusion.85
  133.5 1.6 fusion.85
  135.0 2.5 add_convert_fusion
  137.9 1.8 fusion.41
  139.7 1.8 fusion.39
  141.5 1.8 fusion.30
  143.3 4.6 %fusion.10 = f32[4,512,256]{1,2,0:T(8,128)} fusion(f32[4,512]{1,0:T(4,128)S(1)} %bitcast.109, pred[512,512]{1,0:T(8,128)(4,1)S(1)} %iota_compare_fusion, bf16[512,4,256]{2,1,0:T(4,128)(2,1)} %param.13, bf16[512,4,256]{2,1,0:T(4,128)(2,1)S(1)} %copy-done, bf16[512,4,256]{2,1,0:T(4,128)(2,1)S(1)} %copy-done.2), kind=kOutput, calls=%fused_computation.20 | convolution fusion | flops 1078984704 | bytes 5513216 | tf_op jit(solution)/shard_map/hnm,mhe->nhe/dot_general | solution.py:55
  147.9 1.3 fusion.29
  149.3 0.5 fusion.34
  150.3 0.7 copy-done.3
  151.0 0.6 copy-done.4
  151.6 0.6 copy-done.5
  152.2 2.1 fusion.8
  156.0 34.7 %all-gather.14.cloned.1.call-done = bf16[64,256,256]{2,1,0:T(8,128)(2,1)} async-done(((bf16[4,256,256]{2,1,0:T(8,128)(2,1)}), bf16[64,256,256]{2,1,0:T(8,128)(2,1)}) %all-gather.14.cloned.1.call-update) | async-done | bytes 8388624 | tf_op jit(solution)/shard_map/all_gather | solution.py:127
  190.7 12.6 %fusion.1 = bf16[16,4,256,256]{3,2,1,0:T(8,128)(2,1)} fusion(bf16[16,4,256,256]{3,2,1,0:T(8,128)(2,1)} %bitcast.99), kind=kLoop, calls=%fused_computation.6 | loop fusion | flops 16777216 | bytes 16777216 | tf_op jit(solution)/shard_map/convert_element_type | solution.py:30
  203.4 6.6 %fusion.47 = f32[16,4,256,4,4]{2,4,3,1,0:T(4,128)} fusion(bf16[16,4,256,256,1]{3,2,4,1,0:T(8,128)(2,1)} %bitcast.100, bf16[16,4,4,4,256]{4,3,2,1,0:T(4,128)(2,1)S(1)} %reshape.127), kind=kOutput, calls=%fused_computation.61 | convolution fusion | flops 134217728 | bytes 9961472 | tf_op jit(solution)/shard_map/jcthd,jhde->jcthe/dot_general | solution.py:39
  210.0 12.5 %fusion.5 = f32[16,4,256,4,4]{2,4,3,1,0:T(4,128)} fusion(bf16[16,4,256,256]{3,2,1,0:T(8,128)(2,1)} %fusion.1, bf16[16,4,256,256]{3,2,1,0:T(8,128)(2,1)} %bitcast.101, bf16[16,4,4,4,256]{4,3,2,1,0:T(4,128)(2,1)S(1)} %reshape.127), kind=kOutput, calls=%fused_computation.10 | convolution fusion | flops 159383552 | bytes 18350080 | tf_op jit(solution)/shard_map/jcthd,jhde->jcthe/dot_general | solution.py:41
  222.5 5.3 %fusion.17 = f32[16,4,4,4,256]{4,2,1,3,0:T(4,128)S(1)} fusion(f32[16,4,256,4,4]{2,4,3,1,0:T(4,128)} %fusion.5, f32[16,4,256,4,4]{2,4,3,1,0:T(4,128)} %fusion.47, bf16[16,4,256,256]{3,2,1,0:T(8,128)(2,1)} %fusion.1, bf16[16,4,4,4,256]{4,3,2,1,0:T(4,128)(2,1)S(1)} %reshape.127), kind=kOutput, calls=%fused_computation.24 | convolution fusion | flops 134742016 | bytes 12058624 | tf_op jit(solution)/shard_map/jcthd,jhde->jcthe/dot_general | solution.py:40
  227.7 0.7 copy.77
  228.5 0.9 gather_fusion
  229.3 0.5 fusion.21
  230.0 0.7 copy.93
  230.8 70.3 %all-gather.8.cloned.1.call-done = bf16[512,8192]{0,1:T(8,128)(2,1)} async-done(((bf16[512,1024]{0,1:T(8,128)(2,1)}), bf16[512,8192]{0,1:T(8,128)(2,1)}) %all-gather.8.cloned.1.call-update) | async-done | bytes 8388624 | tf_op jit(solution)/shard_map/all_gather | solution.py:111
  301.1 15.6 %convolution_convert_fusion.1 = bf16[512,1024]{1,0:T(8,128)(2,1)} fusion(bf16[512,8192]{0,1:T(8,128)(2,1)} %all-gather.8.cloned.1.call-done, bf16[8192,1024]{1,0:T(8,128)(2,1)} %param.21), kind=kOutput, calls=%fused_computation.19 | convolution fusion | flops 8590458880 | bytes 26214400 | tf_op jit(solution)/shard_map/dot_general | solution.py:109
  316.7 39.1 %all-gather.10.cloned.1.call-done = bf16[128,8192]{1,0:T(8,128)(2,1)} async-done(((bf16[128,1024]{1,0:T(8,128)(2,1)}), bf16[128,8192]{1,0:T(8,128)(2,1)}) %all-gather.10.cloned.1.call-update) | async-done | bytes 2097168 | tf_op jit(solution)/shard_map/all_gather | solution.py:151
  355.8 8.8 %convolution_convert_fusion.2 = bf16[128,1024]{1,0:T(8,128)(2,1)S(1)} fusion(bf16[128,8192]{1,0:T(8,128)(2,1)} %all-gather.10.cloned.1.call-done, bf16[8192,1024]{1,0:T(8,128)(2,1)} %param.21), kind=kOutput, calls=%fused_computation.28 | convolution fusion | flops 2147614720 | bytes 19136512 | tf_op jit(solution)/shard_map/dot_general | solution.py:109
  364.6 0.8 reshape.130
  (76 shorter events, 3.8 us)
Async XLA Ops:
  7.2 6.7 %copy-start = (bf16[512,4,256]{2,1,0:T(4,128)(2,1)S(1)}, bf16[512,4,256]{2,1,0:T(4,128)(2,1)}, u32[]{:S(2)}) copy-start(bf16[512,4,256]{2,1,0:T(4,128)(2,1)} %param.14) | copy-start | bytes 3145732
  7.2 103.7 %all-gather.12.cloned.1.call-start = ((), (), s32[]{:S(2)}) async-start(), calls=%async_computation.2 | async-start | bytes 17825792 | tf_op jit(solution)/shard_map/all_gather | solution.py:11
  15.4 175.3 %all-gather.14.cloned.1.call-start = ((), (), s32[]{:S(2)}) async-start(), calls=%async_computation.3 | async-start | bytes 8912896 | tf_op jit(solution)/shard_map/all_gather | solution.py:127
  135.0 2.8 copy-start.2
  137.6 163.5 %all-gather.8.cloned.1.call-start = ((), (), s32[]{:S(2)}) async-start(), calls=%async_computation | async-start | bytes 9437184 | tf_op jit(solution)/shard_map/all_gather | solution.py:111
  147.9 1.9 copy-start.6
  147.9 2.4 copy-start.7
  149.2 1.7 copy-start.3
  149.2 2.4 copy-start.4
  149.3 3.0 copy-start.5
  152.2 2.4 copy-start.8
  152.2 2.6 copy-start.10
  152.2 3.5 copy-start.9
  154.4 201.4 %all-gather.10.cloned.1.call-start = ((), (), s32[]{:S(2)}) async-start(), calls=%async_computation.1 | async-start | bytes 2359296 | tf_op jit(solution)/shard_map/all_gather | solution.py:151
  222.5 6.9 %copy-start.11 = (bf16[32,4,4,256]{3,2,1,0:T(4,128)(2,1)S(1)}, bf16[32,4,4,256]{3,2,1,0:T(4,128)(2,1)}, u32[]{:S(2)}) copy-start(bf16[32,4,4,256]{3,2,1,0:T(4,128)(2,1)} %param.19) | copy-start | bytes 786436
  222.5 6.9 %copy-start.12 = (bf16[32,4,4,256]{3,2,1,0:T(4,128)(2,1)S(1)}, bf16[32,4,4,256]{3,2,1,0:T(4,128)(2,1)}, u32[]{:S(2)}) copy-start(bf16[32,4,4,256]{3,2,1,0:T(4,128)(2,1)} %param.18) | copy-start | bytes 786436
  355.8 9.6 %copy-start.1 = (bf16[512,4,256]{2,1,0:T(4,128)(2,1)S(1)}, bf16[512,4,256]{2,1,0:T(4,128)(2,1)}, u32[]{:S(2)}) copy-start(bf16[512,4,256]{2,1,0:T(4,128)(2,1)} %param.14) | copy-start | bytes 3145732
Sparse Core Ops, SparseCore 0:
  15.5 95.3 all-gather.11
  137.7 52.9 all-gather.13
  193.7 107.3 all-gather.7
  303.8 51.9 all-gather.9
where the time goes:
time: 373 us; the launch traced here: 372 us
  waiting for transfers between devices  211 us (57%)
  matrix products  64.5 us (17%)
  other arithmetic  43.6 us (12%)
  blocking collectives  28.4 us (8%)
  between operations  14.7 us (4%)
  local copies, waits for them, and re-layouts  8.8 us (2%)
    all_gather x1, waiting for transfers between devices, shards(): lax.all_gather(retention, 'head', axis=1, tiled=True)  70.3 us
    all_gather x1, waiting for transfers between devices, entering(): pieces = jax.tree.map(lambda part: lax.all_gather(part, axis), value)  66.9 us
    all_gather x1, waiting for transfers between devices, shards(): lax.all_gather(step_flat, 'head', axis=1, tiled=True)  39.1 us
    all_gather x1, waiting for transfers between devices, shards(): lax.all_gather(as_sent(final_state[None]), 'ctx', axis=0, tiled=True)  34.7 us
    unnamed x1, blocking collectives  28.4 us
    dot_general x2, matrix products, project_into(): return jnp.dot(shard_piece, w_out, preferred_element_type=jnp.float32)  24.4 us
    select_n x15, other arithmetic, step(): jnp.where(position < mine, new, old)  23.5 us
    dot_general x2, matrix products, exact_read(): jnp.einsum(form, query_rows, parts[2], preferred_element_type=jnp.float32)  14.3 us
  transfers between devices with their start and end apart: 4, of which 4 were waited for; matrix products, arithmetic and copies ran while one was open for 19% of the time, Pallas kernels for 0%

commit v1 on v0

--- a/solution.py
+++ b/solution.py
@@ -121,11 +121,13 @@
     selector = (jnp.arange(sections * CAP)[:, None] == slot_ids[None, :]).astype(jnp.bfloat16)
     packed = jnp.dot(selector, q_step.reshape(row_count, -1), preferred_element_type=jnp.float32)
     packed = packed.astype(jnp.bfloat16).reshape(sections, CAP, step_count, heads_here, head_dim)
-    reads = exact_read(
-        "jcthd,jhde->jcthe",
-        packed,
-        lax.all_gather(as_sent(final_state[None]), "ctx", axis=0, tiled=True),
-    )
+
+    def use_series_on(local_x):
+        return jnp.concatenate(
+            lax.all_to_all(jnp.stack(lax.axis_size("ctx") * [local_x]), "ctx", 0, 0), axis=0
+        )
+
+    reads = exact_read("jcthd,jhde->jcthe", packed, use_series_on(as_sent(final_state[None])))
     slot_reads = reads
     slot_reads = slot_reads.reshape(sections * CAP, step_count, heads_here, head_dim)
     prefix_reads = jnp.take(slot_reads, slot_ids, axis=0)

time: 373 us -> 454 us (1.22)
  waiting for transfers between devices: 211 us -> 293 us
  matrix products: 64.5 us -> 56.1 us
  local copies, waits for them, and re-layouts: 8.8 us -> 14.9 us
  starting transfers between devices: 0.34 us -> 5.49 us
    all_to_all x0 -> x1, waiting for transfers between devices: none -> 90.8 us  [use_series_on(): lax.all_to_all(jnp.stack(lax.axis_size('ctx') * [local_x]), 'ctx', 0, 0)]
    all_gather x1 -> x0, waiting for transfers between devices: 34.7 us -> none  [shards(): lax.all_gather(as_sent(final_state[None]), 'ctx', axis=0, tiled=True)]
    all_gather x1, waiting for transfers between devices: 70.3 us -> 98.4 us  [shards(): lax.all_gather(retention, 'head', axis=1, tiled=True)]
    all_to_all x0 -> x1, starting transfers between devices: none -> 5.19 us  [use_series_on(): lax.all_to_all(jnp.stack(lax.axis_size('ctx') * [local_x]), 'ctx', 0, 0)]
  transfers between devices with their start and end apart: 4 -> 4, of which waited for: 4 -> 4; matrix products, arithmetic and copies ran while one was open for 19% -> 6% of each run, Pallas kernels for 0% -> 0%
where the time goes in v1:
time: 454 us; the launch traced here: 453 us
  waiting for transfers between devices  293 us (65%)
  matrix products  56.1 us (12%)
  other arithmetic  40.2 us (9%)
  blocking collectives  28.4 us (6%)
  local copies, waits for them, and re-layouts  14.9 us (3%)
  between operations  14.7 us (3%)
  starting transfers between devices  5.49 us (1%)
    all_gather x1, waiting for transfers between devices, shards(): lax.all_gather(retention, 'head', axis=1, tiled=True)  98.4 us
    all_to_all x1, waiting for transfers between devices, use_series_on(): lax.all_to_all(jnp.stack(lax.axis_size('ctx') * [local_x]), 'ctx', 0, 0)  90.8 us
    all_gather x1, waiting for transfers between devices, entering(): pieces = jax.tree.map(lambda part: lax.all_gather(part, axis), value)  67 us
    all_gather x1, waiting for transfers between devices, shards(): lax.all_gather(step_flat, 'head', axis=1, tiled=True)  36.6 us
    unnamed x1, blocking collectives  28.4 us
    dot_general x2, matrix products, project_into(): return jnp.dot(shard_piece, w_out, preferred_element_type=jnp.float32)  24.4 us
    select_n x15, other arithmetic, step(): jnp.where(position < mine, new, old)  23.5 us
    convert_element_type x3, other arithmetic, split_state(): middle_part = rest.astype(jnp.bfloat16)  9.77 us
  transfers between devices with their start and end apart: 4, of which 4 were waited for; matrix products, arithmetic and copies ran while one was open for 6% of the time, Pallas kernels for 0%

profile of v1, /device:TPU:1, one launch (start us, length us, event | category | flops | bytes accessed | tf_op | source)
XLA Modules:
  0.0 453.1 jit_solution(10515728223359039443)
XLA Ops:
  7.2 0.8 reshape.129
  8.0 1.2 reduce-window.6
  10.1 1.8 multiply_convert_fusion.1
  11.8 1.2 dynamic-slice
  13.8 1.5 convolution_add_fusion
  15.4 28.4 %all-reduce = f32[64]{0:T(128)S(1)} all-reduce(f32[64]{0:T(128)S(1)} %get-tuple-element.133), channel_id=2, replica_groups=mesh['ctx'=16,'head'=8] {'ctx'}, use_global_device_ids=true, to_apply=%add | all-reduce | flops 64 | bytes 512
  43.9 67.0 %all-gather.10.cloned.1.call-done = f32[64,256,256]{2,1,0:T(8,128)} async-done(((f32[4,256,256]{2,1,0:T(8,128)}), f32[64,256,256]{2,1,0:T(8,128)}) %all-gather.10.cloned.1.call-update) | async-done | bytes 16777232 | tf_op jit(solution)/shard_map/all_gather | solution.py:11
  110.9 24.2 %while.14 = (s32[]{:T(128)}, f32[4,256,256]{2,1,0:T(8,128)S(1)}, s32[]{:T(128)}, f32[16,4]{1,0:T(8,128)S(1)}, f32[16,4,256,256]{3,2,1,0:T(8,128)}, /*index=5*/s32[]{:T(128)}, s32[]{:T(128)}) while((s32[]{:T(128)}, f32[4,256,256]{2,1,0:T(8,128)S(1)}, s32[]{:T(128)}, f32[16,4]{1,0:T(8,128)S(1)}, f32[16,4,256,256]{3,2,1,0:T(8,128)}, ...), condition=%wide.region_3.4_spmd.clone, body=%wide.region_2.3_spmd.clone.sunk | while | flops 1048580 | bytes 3145881 | solution.py:20
  110.9 1.6 fusion.86
  112.6 1.6 fusion.86
  114.2 1.6 fusion.86
  115.8 1.6 fusion.86
  117.4 1.6 fusion.86
  119.1 1.6 fusion.86
  120.7 1.6 fusion.86
  122.3 1.6 fusion.86
  123.9 1.6 fusion.86
  125.5 1.6 fusion.86
  127.1 1.6 fusion.86
  128.7 1.6 fusion.86
  130.3 1.6 fusion.86
  131.9 1.6 fusion.86
  133.5 1.6 fusion.86
  135.1 1.0 add_convert_fusion
  136.1 4.3 stack.2
  140.4 5.2 %all-to-all-start = ((bf16[16,1,4,256,256]{4,3,2,1,0:T(8,128)(2,1)}), bf16[16,1,4,256,256]{4,3,2,1,0:T(8,128)(2,1)}, u32[]{:S(2)}, u32[]{:S(2)}) async-start(bf16[16,1,4,256,256]{4,3,2,1,0:T(8,128)(2,1)} %stack.2), calls=%async_computation | async-start | bytes 16777216 | tf_op jit(solution)/shard_map/all_to_all | solution.py:127
  147.6 1.2 and_bitcast_fusion
  149.4 90.8 %all-to-all-done = bf16[16,1,4,256,256]{4,3,2,1,0:T(8,128)(2,1)} async-done(((bf16[16,1,4,256,256]{4,3,2,1,0:T(8,128)(2,1)}), bf16[16,1,4,256,256]{4,3,2,1,0:T(8,128)(2,1)}, u32[]{:S(2)}, u32[]{:S(2)}) %all-to-all-start) | async-done | bytes 8388640 | tf_op jit(solution)/shard_map/all_to_all | solution.py:127
  240.2 8.4 %fusion.1 = bf16[16,4,256,256]{3,2,1,0:T(8,128)(2,1)S(1)} fusion(bf16[16,4,256,256]{3,2,1,0:T(8,128)(2,1)} %bitcast.13, bf16[16,1,4,256,256]{4,3,2,1,0:T(8,128)(2,1)} %all-to-all-done), kind=kLoop, calls=%fused_computation.6 | loop fusion | flops 16777216 | bytes 25165824 | tf_op jit(solution)/shard_map/convert_element_type | solution.py:30
  248.6 1.4 fusion.3
  250.0 7.9 %fusion.7 = f32[16,4,256,4,4]{2,4,3,1,0:T(4,128)S(1)} fusion(bf16[16,4,256,256]{3,2,1,0:T(8,128)(2,1)S(1)} %fusion.1, bf16[16,4,256,256]{3,2,1,0:T(8,128)(2,1)} %bitcast.13, bf16[16,4,4,4,256]{4,3,2,1,0:T(4,128)(2,1)S(1)} %reshape.134, bf16[16,1,4,256,256]{4,3,2,1,0:T(8,128)(2,1)} %all-to-all-done), kind=kOutput, calls=%fused_computation.12 | convolution fusion | flops 159383552 | bytes 26738688 | tf_op jit(solution)/shard_map/jcthd,jhde->jcthe/dot_general | solution.py:41
  257.9 4.7 %fusion.19 = f32[16,4,4,4,256]{4,2,1,3,0:T(4,128)S(1)} fusion(f32[16,4,256,4,4]{2,4,3,1,0:T(4,128)S(1)} %fusion.7, f32[16,4,256,4,4]{2,4,3,1,0:T(4,128)S(1)} %fusion.3, bf16[16,1,4,256,256]{4,3,2,1,0:T(8,128)(2,1)} %all-to-all-done, bf16[16,4,4,4,256]{4,3,2,1,0:T(4,128)(2,1)S(1)} %reshape.134), kind=kOutput, calls=%fused_computation.26 | convolution fusion | flops 134742016 | bytes 12058624 | tf_op jit(solution)/shard_map/jcthd,jhde->jcthe/dot_general | solution.py:39
  262.6 0.7 copy.77
  263.3 1.7 gather_fusion
  265.0 2.5 fusion.23
  267.5 1.1 copy.84
  268.6 0.7 copy.93
  269.8 1.8 fusion.43
  271.7 1.8 fusion.41
  273.5 1.8 fusion.32
  275.3 4.7 %fusion.12 = f32[4,512,256]{1,2,0:T(8,128)} fusion(f32[4,512]{1,0:T(4,128)S(1)} %bitcast.111, pred[512,512]{1,0:T(8,128)(4,1)S(1)} %iota_compare_fusion, bf16[512,4,256]{2,1,0:T(4,128)(2,1)} %param.13, bf16[512,4,256]{2,1,0:T(4,128)(2,1)S(1)} %copy-done, bf16[512,4,256]{2,1,0:T(4,128)(2,1)S(1)} %copy-done.1), kind=kOutput, calls=%fused_computation.22 | convolution fusion | flops 1078984704 | bytes 5513216 | tf_op jit(solution)/shard_map/hnm,mhe->nhe/dot_general | solution.py:55
  279.9 1.3 fusion.31
  284.2 2.1 fusion.10
  286.4 36.6 %all-gather.8.cloned.1.call-done = bf16[128,8192]{1,0:T(8,128)(2,1)} async-done(((bf16[128,1024]{1,0:T(8,128)(2,1)}), bf16[128,8192]{1,0:T(8,128)(2,1)}) %all-gather.8.cloned.1.call-update) | async-done | bytes 2097168 | tf_op jit(solution)/shard_map/all_gather | solution.py:153
  322.9 8.7 %convolution_convert_fusion.2 = bf16[128,1024]{1,0:T(8,128)(2,1)S(1)} fusion(bf16[128,8192]{1,0:T(8,128)(2,1)} %all-gather.8.cloned.1.call-done, bf16[8192,1024]{1,0:T(8,128)(2,1)} %param.21), kind=kOutput, calls=%fused_computation.30 | convolution fusion | flops 2147614720 | bytes 19136512 | tf_op jit(solution)/shard_map/dot_general | solution.py:109
  331.7 0.8 reshape.137
  332.5 98.4 %all-gather.6.cloned.1.call-done = bf16[512,8192]{0,1:T(8,128)(2,1)} async-done(((bf16[512,1024]{0,1:T(8,128)(2,1)}), bf16[512,8192]{0,1:T(8,128)(2,1)}) %all-gather.6.cloned.1.call-update) | async-done | bytes 8388624 | tf_op jit(solution)/shard_map/all_gather | solution.py:111
  430.9 15.7 %convolution_convert_fusion.1 = bf16[512,1024]{1,0:T(8,128)(2,1)} fusion(bf16[512,8192]{0,1:T(8,128)(2,1)} %all-gather.6.cloned.1.call-done, bf16[8192,1024]{1,0:T(8,128)(2,1)} %param.21), kind=kOutput, calls=%fused_computation.21 | convolution fusion | flops 8590458880 | bytes 26214400 | tf_op jit(solution)/shard_map/dot_general | solution.py:109
  (74 shorter events, 7.2 us)
Async XLA Ops:
  7.2 6.7 %copy-start = (bf16[512,4,256]{2,1,0:T(4,128)(2,1)S(1)}, bf16[512,4,256]{2,1,0:T(4,128)(2,1)}, u32[]{:S(2)}) copy-start(bf16[512,4,256]{2,1,0:T(4,128)(2,1)} %param.14) | copy-start | bytes 3145732
  7.2 103.7 %all-gather.10.cloned.1.call-start = ((), (), s32[]{:S(2)}) async-start(), calls=%async_computation.3 | async-start | bytes 17825792 | tf_op jit(solution)/shard_map/all_gather | solution.py:11
  110.9 24.2 %copy-start.6 = (f32[4,256,256]{2,1,0:T(8,128)S(1)}, f32[4,256,256]{2,1,0:T(8,128)}, u32[]{:S(2)}) copy-start(f32[4,256,256]{2,1,0:T(8,128)} %convolution_add_fusion) | copy-start | bytes 3145732
  140.4 5.2 %copy-start.8 = (bf16[32,4,4,256]{3,2,1,0:T(4,128)(2,1)S(1)}, bf16[32,4,4,256]{3,2,1,0:T(4,128)(2,1)}, u32[]{:S(2)}) copy-start(bf16[32,4,4,256]{3,2,1,0:T(4,128)(2,1)} %param.17) | copy-start | bytes 786436
  140.4 5.4 %copy-start.10 = (s32[32,1]{0,1:T(1,128)S(1)}, s32[32,1]{0,1:T(1,128)}, u32[]{:S(2)}) copy-start(s32[32,1]{0,1:T(1,128)} %param.16) | copy-start | bytes 388
  140.4 6.4 %copy-start.9 = (f32[4,4,32]{2,1,0:T(4,128)S(1)}, f32[4,4,32]{2,1,0:T(4,128)}, u32[]{:S(2)}) copy-start(f32[4,4,32]{2,1,0:T(4,128)} %param.20) | copy-start | bytes 6148
  140.4 99.8 %all-to-all-start = ((bf16[16,1,4,256,256]{4,3,2,1,0:T(8,128)(2,1)}), bf16[16,1,4,256,256]{4,3,2,1,0:T(8,128)(2,1)}, u32[]{:S(2)}, u32[]{:S(2)}) async-start(bf16[16,1,4,256,256]{4,3,2,1,0:T(8,128)(2,1)} %stack.2), calls=%async_computation | async-start | bytes 16777216 | tf_op jit(solution)/shard_map/all_to_all | solution.py:127
  145.6 177.3 %all-gather.8.cloned.1.call-start = ((), (), s32[]{:S(2)}) async-start(), calls=%async_computation.2 | async-start | bytes 2359296 | tf_op jit(solution)/shard_map/all_gather | solution.py:153
  146.1 0.7 copy-start.11
  265.0 4.8 %copy-start.1 = (bf16[512,4,256]{2,1,0:T(4,128)(2,1)S(1)}, bf16[512,4,256]{2,1,0:T(4,128)(2,1)}, u32[]{:S(2)}) copy-start(bf16[512,4,256]{2,1,0:T(4,128)(2,1)} %param.12) | copy-start | bytes 3145732
  269.4 161.6 %all-gather.6.cloned.1.call-start = ((), (), s32[]{:S(2)}) async-start(), calls=%async_computation.1 | async-start | bytes 9437184 | tf_op jit(solution)/shard_map/all_gather | solution.py:111
  279.9 1.9 copy-start.5
  279.9 2.4 copy-start.7
  281.2 1.7 copy-start.2
  281.3 2.4 copy-start.3
  281.3 3.0 copy-start.4
Sparse Core Ops, SparseCore 0:
  15.5 95.3 all-gather.9
  269.5 53.4 all-gather.7
  325.9 105.0 all-gather.5
